TPU v7x, 32 devices: a whole 2x2x4 slice. The times are simulated.
32 devices in a mesh: hap: 2 (over x), snp: 16 (over z, y, core).
Axes of the slice: x: 2, y: 2, z: 4, core: 2. Of those that a mesh axis runs over, the one named last changes fastest.
Arguments:
- packed_panel: int32 [96, 16384], P('hap', 'snp'), may hold values from 0 to 8191, as said below
- components: bfloat16 [64, 1248], P(None, 'hap'), may hold values from -0.15625 to 0.15625
- bounds: int32 [2, 16384], P(None, 'snp'), may hold values from 0 to 16383, as said below
- band_width: int32 [16384], P('snp'), may hold values from 1 to 256
Outputs:
- ld_scores: float32 [16384], P('snp')
Inputs may be any that keep to these rules, and one draw needn't show every extreme that they name: Bit j of packed_panel[w, s] (j from 0 to 12) is the allele of haplotype 13 w + j at SNP s; higher bits are zero. LD blocks are consecutive runs of 1 to 2048 SNPs that cover all SNPs in order; bounds[0, s] and bounds[1, s] are the first and last SNP of the block holding s.
All inputs are finite; a program needn't handle non-finite values.
Results may differ from a plain program's by a relative error of at most 0.00074.
Values may be sent and summed in bfloat16 or wider, within the bound.
No kernel may reach another device: no remote copies, remote signals or barrier semaphores. Data moves between devices by JAX's collectives and lax.ppermute only.
A program may use at most 64 MiB of HBM per device.

v0:
```python
import jax
import jax.numpy as jnp
from jax import lax
from jax.sharding import PartitionSpec as P

epsilon = 1e-06


def padded_2(block, sides, width):
    for axis, dim in sides:
        count = lax.axis_size(axis)
        forward = [(i, i + 1) for i in range(count - 1)]
        backward = [(target, source) for source, target in forward]
        low = lax.ppermute(
            lax.slice_in_dim(block, block.shape[dim] - width, None, axis=dim), axis, forward
        )
        high = lax.ppermute(lax.slice_in_dim(block, 0, width, axis=dim), axis, backward)
        block = jnp.concatenate([low, block, high], axis=dim)
    return block


def unpack(packed):
    shifts = jnp.arange(13, dtype=jnp.int32)
    bit_values = jnp.bitwise_and(jnp.right_shift(packed[:, None, :], shifts[None, :, None]), 1)
    return bit_values.reshape(packed.shape[0] * 13, packed.shape[1]).astype(jnp.bfloat16)


def project(components, packed_panel):
    column_count = packed_panel.shape[1]
    block_size = min(256, column_count)
    zeroed = jnp.zeros((components.shape[0], column_count), jnp.float32)

    def add_block(block_index, accumulated):
        packed = lax.dynamic_slice_in_dim(packed_panel, block_index * block_size, block_size, 1)
        product = jnp.dot(components, unpack(packed), preferred_element_type=jnp.float32)
        return lax.dynamic_update_slice_in_dim(accumulated, product, block_index * block_size, 1)

    return lax.fori_loop(0, column_count // block_size, add_block, zeroed)


def standardize(factor):
    average = jnp.mean(factor, axis=1, keepdims=True)
    centered = factor - average
    variance = jnp.mean(centered * centered, axis=1, keepdims=True)
    return (centered * lax.rsqrt(variance + epsilon)).astype(jnp.bfloat16)


def band_scores(padded, inverse, bounds, band_width, offset, start_row, row_count, reach_width):
    component_count = padded.shape[0]
    block_size = min(256, row_count)

    def block_scores(block_index):
        first_row = start_row + block_index * block_size
        row_part = lax.dynamic_slice_in_dim(padded, first_row + reach_width, block_size, 1)
        column_part = lax.dynamic_slice_in_dim(padded, first_row, block_size + 2 * reach_width, 1)
        inverse_rows = lax.dynamic_slice_in_dim(inverse, first_row + reach_width, block_size, 0)
        inverse_columns = lax.dynamic_slice_in_dim(
            inverse, first_row, block_size + 2 * reach_width, 0
        )
        block_first = lax.dynamic_slice_in_dim(bounds[0], first_row, block_size, 0)
        block_last = lax.dynamic_slice_in_dim(bounds[1], first_row, block_size, 0)
        row_reach = lax.dynamic_slice_in_dim(band_width, first_row, block_size, 0)
        inner_products = lax.dot_general(
            row_part, column_part, (((0,), (0,)), ((), ())), preferred_element_type=jnp.float32
        )
        correlation = (
            inner_products
            * (1.0 / component_count)
            * inverse_rows[:, None]
            * inverse_columns[None, :]
        )
        row_position = offset + first_row + jnp.arange(block_size, dtype=jnp.int32)
        column_position = (
            offset
            + first_row
            - reach_width
            + jnp.arange(block_size + 2 * reach_width, dtype=jnp.int32)
        )
        window_low = jnp.maximum(block_first, row_position - row_reach)
        window_high = jnp.minimum(block_last, row_position + row_reach)
        inside = (
            (column_position[None, :] >= window_low[:, None])
            & (column_position[None, :] <= window_high[:, None])
            & (column_position[None, :] != row_position[:, None])
        )
        squared_sum = jnp.sum(jnp.where(inside, correlation * correlation, 0.0), axis=1)
        window_count = jnp.sum(inside.astype(jnp.float32), axis=1)
        return component_count * squared_sum / jnp.maximum(window_count, 1.0)

    blocks = jnp.arange(row_count // block_size, dtype=jnp.int32)
    return lax.map(block_scores, blocks).reshape(row_count)


def on_device(packed_panel, components, bounds, band_width):
    partial_factor = project(components, packed_panel)
    column_count = partial_factor.shape[1]
    factor = lax.psum(partial_factor, "hap")
    component_rows = lax.all_to_all(factor, "snp", split_axis=0, concat_axis=1, tiled=True)
    scaled = standardize(component_rows)
    normed = lax.all_to_all(scaled, "snp", split_axis=1, concat_axis=0, tiled=True)
    reach_width = column_count // 4
    padded = padded_2(normed, (("snp", 1),), reach_width)
    inverse = lax.rsqrt(jnp.mean(jnp.square(padded.astype(jnp.float32)), axis=0) + epsilon)
    offset = lax.axis_index("snp") * column_count
    share_rows = column_count // lax.axis_size("hap")
    own_scores = band_scores(
        padded,
        inverse,
        bounds,
        band_width,
        offset,
        lax.axis_index("hap") * share_rows,
        share_rows,
        reach_width,
    )
    return lax.all_gather(own_scores, "hap", axis=0, tiled=True)


def solution(mesh):
    in_specs = (P("hap", "snp"), P(None, "hap"), P(None, "snp"), P("snp"))
    out_specs = P("snp")
    return jax.shard_map(
        on_device, mesh=mesh, in_specs=in_specs, out_specs=out_specs, check_vma=False
    )
```

profile of v0, /device:TPU:13, one launch (start us, length us, event | category | flops | bytes accessed | tf_op | source)
XLA Modules:
  0.0 91.0 jit_solution(2346714453307130350)
XLA Ops:
  6.6 0.9 copy-done
  7.4 5.6 %while.25 = (s32[]{:T(128)}, f32[64,1024]{1,0:T(8,128)S(1)}, s32[48,1024]{1,0:T(8,128)}, bf16[64,624]{1,0:T(8,128)(2,1)S(1)}, s32[]{:T(128)}, /*index=5*/s32[]{:T(128)}, s32[]{:T(128)}, s32[]{:T(128)}) while((s32[]{:T(128)}, f32[64,1024]{1,0:T(8,128)S(1)}, s32[48,1024]{1,0:T(8,128)}, bf16[64,624]{1,0:T(8,128)(2,1)S(1)}, s32[]{:T(128)}, ...), condition=%wide.region_1.0_spmd, body=%wide.region_0.0_spmd.sunk | while | flops 20926468 | bytes 2862539 | solution.py:38
  7.4 0.8 constant_dynamic-slice_fusion.6
  8.5 0.3 fusion.22
  8.8 0.8 constant_dynamic-slice_fusion.6
  9.9 0.3 fusion.22
  10.3 0.8 constant_dynamic-slice_fusion.6
  11.4 0.3 fusion.22
  11.7 0.8 constant_dynamic-slice_fusion.6
  12.8 0.3 fusion.22
  13.1 0.8 all_to_all.22
  13.9 24.1 %all-reduce.2.cloned.1.call-done = f32[16,4,1024]{2,1,0:T(4,128)} async-done(((f32[16,4,1024]{2,1,0:T(4,128)}), f32[16,4,1024]{2,1,0:T(4,128)}) %all-reduce.2.cloned.1.call-update) | async-done | bytes 262160 | tf_op jit(solution)/shard_map/psum | solution.py:97
  37.9 14.8 %all_to_all.29 = f32[16,4,1024]{2,1,0:T(4,128)S(1)} all-to-all(f32[16,4,1024]{2,1,0:T(4,128)} %all-reduce.2.cloned.1.call-done), channel_id=1, replica_groups=mesh['hap'=2,'snp'=16] {'snp'}, dimensions={0} | all-to-all | bytes 524288 | tf_op jit(solution)/shard_map/all_to_all | solution.py:98
  52.7 0.3 reduce_sum.51
  53.0 0.3 multiply_reduce_fusion.1
  53.3 0.1 fusion.11
  53.5 9.9 %all_to_all.30 = bf16[4,16,1024]{2,0,1:T(4,128)(2,1)S(1)} all-to-all(bf16[4,16,1024]{2,0,1:T(4,128)(2,1)S(1)} %fusion.11), channel_id=1, replica_groups=mesh['hap'=2,'snp'=16] {'snp'}, dimensions={1} | all-to-all | bytes 262144 | tf_op jit(solution)/shard_map/all_to_all | solution.py:100
  63.4 3.7 %collective-permute-start = (bf16[64,256]{1,0:T(8,128)(2,1)S(1)}, bf16[64,256]{1,0:T(8,128)(2,1)S(1)}, u32[]{:S(2)}, u32[]{:S(2)}) collective-permute-start(bf16[64,256]{1,0:T(8,128)(2,1)S(1)} %get-tuple-element.232), channel_id=1, source_target_pairs={{0,1},{1,2},{2,3},{3,4},{4,5},{5,6},{6,7},{7,8},{8,9},{9,10},{10,1... | collective-permute-start | bytes 98312 | tf_op jit(solution)/shard_map/ppermute | solution.py:14
  67.1 1.9 %collective-permute-start.1 = (bf16[64,256]{1,0:T(8,128)(2,1)S(1)}, bf16[64,256]{1,0:T(8,128)(2,1)S(1)}, u32[]{:S(2)}, u32[]{:S(2)}) collective-permute-start(bf16[64,256]{1,0:T(8,128)(2,1)S(1)} %get-tuple-element.231), channel_id=1, source_target_pairs={{1,0},{2,1},{3,2},{4,3},{5,4},{6,5},{7,6},{8,7},{9,8},{10,9},{11,1... | collective-permute-start | bytes 98312 | tf_op jit(solution)/shard_map/ppermute | solution.py:17
  69.1 4.2 %collective-permute-done.1 = bf16[64,256]{1,0:T(8,128)(2,1)S(1)} collective-permute-done((bf16[64,256]{1,0:T(8,128)(2,1)S(1)}, bf16[64,256]{1,0:T(8,128)(2,1)S(1)}, u32[]{:S(2)}, u32[]{:S(2)}) %collective-permute-start.1) | collective-permute-done | bytes 32800 | tf_op jit(solution)/shard_map/ppermute | solution.py:17
  73.4 0.7 copy-done.1
  74.0 6.3 %while.26 = (s32[]{:T(128)}, f32[2,256]{1,0:T(2,128)S(1)}, s32[2]{0:T(128)S(1)}, s32[]{:T(128)}, s32[]{:T(128)}, /*index=5*/s32[2,1024]{1,0:T(2,128)S(1)}, s32[1...) while((s32[]{:T(128)}, f32[2,256]{1,0:T(2,128)S(1)}, ...), condition=%wide.region_9.10_spmd, body=%wide.region_6.9_spmd.sunk | while | flops 28510736 | bytes 194922 | solution.py:91
  74.0 0.6 dynamic_slice.80
  75.4 0.8 subtract_maximum_fusion.2
  76.3 0.5 fusion.26
  76.8 0.3 convert_reduce_fusion.2
  77.2 0.6 dynamic_slice.80
  78.5 0.8 subtract_maximum_fusion.2
  79.5 0.5 fusion.26
  80.0 0.3 convert_reduce_fusion.2
  80.4 3.2 %all-gather = f32[2,1,512]{2,1,0:T(1,128)S(1)} all-gather(f32[1,1,512]{2,1,0:T(1,128)S(1)} %reshape.97), channel_id=1, replica_groups=mesh['hap'=2,'snp'=16] {'hap'}, dimensions={0}, use_global_device_ids=true | all-gather | bytes 6144 | tf_op jit(solution)/shard_map/all_gather | solution.py:116
  83.6 0.6 copy.23
  (50 shorter events, 1.7 us)
Async XLA Ops:
  6.5 31.4 %all-reduce.2.cloned.1.call-start = ((), (), s32[]{:S(2)}) async-start(), calls=%async_computation.2 | async-start | bytes 524288 | tf_op jit(solution)/shard_map/psum | solution.py:97
  6.5 0.9 copy-start
  63.4 5.7 %collective-permute-start = (bf16[64,256]{1,0:T(8,128)(2,1)S(1)}, bf16[64,256]{1,0:T(8,128)(2,1)S(1)}, u32[]{:S(2)}, u32[]{:S(2)}) collective-permute-start(bf16[64,256]{1,0:T(8,128)(2,1)S(1)} %get-tuple-element.232), channel_id=1, source_target_pairs={{0,1},{1,2},{2,3},{3,4},{4,5},{5,6},{6,7},{7,8},{8,9},{9,10},{10,1... | collective-permute-start | bytes 98312 | tf_op jit(solution)/shard_map/ppermute | solution.py:14
  67.1 6.1 %collective-permute-start.1 = (bf16[64,256]{1,0:T(8,128)(2,1)S(1)}, bf16[64,256]{1,0:T(8,128)(2,1)S(1)}, u32[]{:S(2)}, u32[]{:S(2)}) collective-permute-start(bf16[64,256]{1,0:T(8,128)(2,1)S(1)} %get-tuple-element.231), channel_id=1, source_target_pairs={{1,0},{2,1},{3,2},{4,3},{5,4},{6,5},{7,6},{8,7},{9,8},{10,9},{11,1... | collective-permute-start | bytes 98312 | tf_op jit(solution)/shard_map/ppermute | solution.py:17
  73.3 0.7 copy-start.1
Sparse Core Ops, SparseCore 0:
  14.0 23.8 all-reduce.1
where the time goes:
time: 91.7 us; the launch traced here: 91 us
  waiting for transfers between devices  28.2 us (31%)
  blocking collectives  27.9 us (30%)
  between operations  13.5 us (15%)
  local copies, waits for them, and re-layouts  8.78 us (10%)
  starting transfers between devices  5.62 us (6%)
  other arithmetic  3.17 us (3%)
  matrix products  2.22 us (2%)
  loops' own time  1.59 us (2%)
    psum x1, waiting for transfers between devices, on_device(): factor = lax.psum(partial_factor, 'hap')  24.1 us
    all_to_all x1, blocking collectives, on_device(): lax.all_to_all(factor, 'snp', split_axis=0, concat_axis=1, tiled=True)  14.8 us
    all_to_all x1, blocking collectives, on_device(): lax.all_to_all(scaled, 'snp', split_axis=1, concat_axis=0, tiled=True)  9.91 us
    ppermute x1, waiting for transfers between devices, padded_2(): lax.ppermute(lax.slice_in_dim(block, 0, width, axis=dim), axis, backward)  4.16 us
    ppermute x1, starting transfers between devices, padded_2(): lax.ppermute(lax.slice_in_dim(block, block.shape[dim] - width, None, axis...  3.7 us
    dynamic_slice x4, local copies, waits for them, and re-layouts, add_block(): lax.dynamic_slice_in_dim(packed_panel, block_index * block_size, block_si...  3.23 us
    all_gather x1, blocking collectives, on_device(): return lax.all_gather(own_scores, 'hap', axis=0, tiled=True)  3.21 us
    unnamed x8, local copies, waits for them, and re-layouts  2.16 us
  transfers between devices with their start and end apart: 3, of which 2 were waited for; matrix products, arithmetic and copies ran while one was open for 0% of the time, Pallas kernels for 0%

commit v1 on v0

--- a/solution.py
+++ b/solution.py
@@ -4,6 +4,21 @@
 from jax.sharding import PartitionSpec as P
 
 epsilon = 1e-06
+
+
+def recast_ranges(mine, k_dim, s0):
+    extra = mine.shape
+    return jnp.moveaxis(
+        mine.reshape(*extra[:k_dim], s0, extra[k_dim] // s0, *extra[k_dim + 1 :]), k_dim, 0
+    )
+
+
+def _track_zones(chunk, at_axis):
+    chunk = jnp.moveaxis(chunk, 0, at_axis)
+    local_now = chunk.shape
+    return chunk.reshape(
+        *local_now[:at_axis], local_now[at_axis] * local_now[at_axis + 1], *local_now[at_axis + 2 :]
+    )
 
 
 def padded_2(block, sides, width):
@@ -95,7 +110,14 @@
     partial_factor = project(components, packed_panel)
     column_count = partial_factor.shape[1]
     factor = lax.psum(partial_factor, "hap")
-    component_rows = lax.all_to_all(factor, "snp", split_axis=0, concat_axis=1, tiled=True)
+    prior, w_next = (lax.psum(1, "snp"), lax.axis_index("snp"))
+    opened = recast_ranges(factor, 0, prior)
+    panels = [opened[w_next]]
+    for dev_i in range(1, prior):
+        outcome_arr = opened[w_next ^ dev_i]
+        panels.append(lax.ppermute(outcome_arr, "snp", [(jj, jj ^ dev_i) for jj in range(prior)]))
+    opened = jnp.stack(panels)[w_next ^ jnp.arange(prior)]
+    component_rows = _track_zones(opened, 1)
     scaled = standardize(component_rows)
     normed = lax.all_to_all(scaled, "snp", split_axis=1, concat_axis=0, tiled=True)
     reach_width = column_count // 4

time: 91.7 us -> 104 us (1.13)
  starting transfers between devices: 5.62 us -> 23.5 us
  blocking collectives: 27.9 us -> 17.5 us
  waiting for transfers between devices: 28.2 us -> 31 us
  local copies, waits for them, and re-layouts: 8.78 us -> 10.6 us
    ppermute x0 -> x15, starting transfers between devices: none -> 18 us  [on_device(): lax.ppermute(outcome_arr, 'snp', [(jj, jj ^ dev_i) for jj in range(prior)])]
    all_to_all x1 -> x0, blocking collectives: 14.8 us -> none  [on_device(): lax.all_to_all(factor, 'snp', split_axis=0, concat_axis=1, tiled=True)]
    all_to_all x1, blocking collectives: 9.91 us -> 14.3 us  [on_device(): lax.all_to_all(scaled, 'snp', split_axis=1, concat_axis=0, tiled=True)]
    ppermute x0 -> x15, waiting for transfers between devices: none -> 2.81 us  [on_device(): lax.ppermute(outcome_arr, 'snp', [(jj, jj ^ dev_i) for jj in range(prior)])]
    unnamed x8 -> x22, local copies, waits for them, and re-layouts: 2.16 us -> 2.27 us
  transfers between devices with their start and end apart: 3 -> 18, of which waited for: 2 -> 5; matrix products, arithmetic and copies ran while one was open for 0% -> 0% of each run, Pallas kernels for 0% -> 0%
where the time goes in v1:
time: 104 us; the launch traced here: 103 us
  waiting for transfers between devices  31 us (30%)
  starting transfers between devices  23.5 us (23%)
  blocking collectives  17.5 us (17%)
  between operations  13.6 us (13%)
  local copies, waits for them, and re-layouts  10.6 us (10%)
  other arithmetic  3.17 us (3%)
  matrix products  2.22 us (2%)
  loops' own time  1.6 us (2%)
    psum x1, waiting for transfers between devices, on_device(): factor = lax.psum(partial_factor, 'hap')  24 us
    ppermute x15, starting transfers between devices, on_device(): lax.ppermute(outcome_arr, 'snp', [(jj, jj ^ dev_i) for jj in range(prior)])  18 us
    all_to_all x1, blocking collectives, on_device(): lax.all_to_all(scaled, 'snp', split_axis=1, concat_axis=0, tiled=True)  14.3 us
    ppermute x1, waiting for transfers between devices, padded_2(): lax.ppermute(lax.slice_in_dim(block, 0, width, axis=dim), axis, backward)  4.16 us
    ppermute x1, starting transfers between devices, padded_2(): lax.ppermute(lax.slice_in_dim(block, block.shape[dim] - width, None, axis...  3.61 us
    dynamic_slice x4, local copies, waits for them, and re-layouts, add_block(): lax.dynamic_slice_in_dim(packed_panel, block_index * block_size, block_si...  3.23 us
    all_gather x1, blocking collectives, on_device(): return lax.all_gather(own_scores, 'hap', axis=0, tiled=True)  3.21 us
    ppermute x15, waiting for transfers between devices, on_device(): lax.ppermute(outcome_arr, 'snp', [(jj, jj ^ dev_i) for jj in range(prior)])  2.81 us
  transfers between devices with their start and end apart: 18, of which 5 were waited for; matrix products, arithmetic and copies ran while one was open for 0% of the time, Pallas kernels for 0%

profile of v1, /device:TPU:13, one launch (start us, length us, event | category | flops | bytes accessed | tf_op | source)
XLA Modules:
  0.0 103.1 jit_solution(7049134473919948288)
XLA Ops:
  6.6 0.9 copy-done
  7.4 5.6 %while.25 = (s32[]{:T(128)}, f32[64,1024]{1,0:T(8,128)S(1)}, s32[48,1024]{1,0:T(8,128)}, bf16[64,624]{1,0:T(8,128)(2,1)S(1)}, s32[]{:T(128)}, /*index=5*/s32[]{:T(128)}, s32[]{:T(128)}, s32[]{:T(128)}) while((s32[]{:T(128)}, f32[64,1024]{1,0:T(8,128)S(1)}, s32[48,1024]{1,0:T(8,128)}, bf16[64,624]{1,0:T(8,128)(2,1)S(1)}, s32[]{:T(128)}, ...), condition=%wide.region_1.0_spmd, body=%wide.region_0.0_spmd.sunk | while | flops 20926468 | bytes 2862547 | solution.py:53
  7.4 0.8 constant_dynamic-slice_fusion.6
  8.8 0.8 constant_dynamic-slice_fusion.6
  10.3 0.8 constant_dynamic-slice_fusion.6
  11.7 0.8 constant_dynamic-slice_fusion.6
  13.1 0.8 reshape.113
  14.0 24.0 %all-reduce.2.cloned.1.call-done = f32[16,4,1024]{2,1,0:T(4,128)} async-done(((f32[16,4,1024]{2,1,0:T(4,128)}), f32[16,4,1024]{2,1,0:T(4,128)}) %all-reduce.2.cloned.1.call-update) | async-done | bytes 262160 | tf_op jit(solution)/shard_map/psum | solution.py:112
  37.9 0.9 dynamic-slice_bitcast_fusion
  38.9 1.3 %collective-permute-start = (f32[4,1024]{1,0:T(4,128)S(1)}, f32[4,1024]{1,0:T(4,128)S(1)}, u32[]{:S(2)}, u32[]{:S(2)}) collective-permute-start(f32[4,1024]{1,0:T(4,128)S(1)} %get-tuple-element.245), channel_id=1, source_target_pairs={{0,1},{1,0},{2,3},{3,2},{4,5},{5,4},{6,7},{7,6},{8,9},{9,8},{10,11... | collective-permute-start | bytes 49160 | tf_op jit(solution)/shard_map/ppermute | solution.py:118
  40.4 1.4 %collective-permute-start.2 = (f32[4,1024]{1,0:T(4,128)S(1)}, f32[4,1024]{1,0:T(4,128)S(1)}, u32[]{:S(2)}, u32[]{:S(2)}) collective-permute-start(f32[4,1024]{1,0:T(4,128)S(1)} %get-tuple-element.243), channel_id=1, source_target_pairs={{0,3},{1,2},{2,1},{3,0},{4,7},{5,6},{6,5},{7,4},{8,11},{9,10},{10,... | collective-permute-start | bytes 49160 | tf_op jit(solution)/shard_map/ppermute | solution.py:118
  42.1 1.5 %collective-permute-start.4 = (f32[4,1024]{1,0:T(4,128)S(1)}, f32[4,1024]{1,0:T(4,128)S(1)}, u32[]{:S(2)}, u32[]{:S(2)}) collective-permute-start(f32[4,1024]{1,0:T(4,128)S(1)} %get-tuple-element.241), channel_id=1, source_target_pairs={{0,5},{1,4},{2,7},{3,6},{4,1},{5,0},{6,3},{7,2},{8,13},{9,12},{10,... | collective-permute-start | bytes 49160 | tf_op jit(solution)/shard_map/ppermute | solution.py:118
  43.9 2.4 %collective-permute-start.6 = (f32[4,1024]{1,0:T(4,128)S(1)}, f32[4,1024]{1,0:T(4,128)S(1)}, u32[]{:S(2)}, u32[]{:S(2)}) collective-permute-start(f32[4,1024]{1,0:T(4,128)S(1)} %get-tuple-element.239), channel_id=1, source_target_pairs={{0,7},{1,6},{2,5},{3,4},{4,3},{5,2},{6,1},{7,0},{8,15},{9,14},{10,... | collective-permute-start | bytes 49160 | tf_op jit(solution)/shard_map/ppermute | solution.py:118
  46.3 2.1 %collective-permute-start.7 = (f32[4,1024]{1,0:T(4,128)S(1)}, f32[4,1024]{1,0:T(4,128)S(1)}, u32[]{:S(2)}, u32[]{:S(2)}) collective-permute-start(f32[4,1024]{1,0:T(4,128)S(1)} %get-tuple-element.238), channel_id=1, source_target_pairs={{0,8},{1,9},{2,10},{3,11},{4,12},{5,13},{6,14},{7,15},{8,0},{9,1},... | collective-permute-start | bytes 49160 | tf_op jit(solution)/shard_map/ppermute | solution.py:118
  49.0 2.1 %collective-permute-start.9 = (f32[4,1024]{1,0:T(4,128)S(1)}, f32[4,1024]{1,0:T(4,128)S(1)}, u32[]{:S(2)}, u32[]{:S(2)}) collective-permute-start(f32[4,1024]{1,0:T(4,128)S(1)} %get-tuple-element.236), channel_id=1, source_target_pairs={{0,10},{1,11},{2,8},{3,9},{4,14},{5,15},{6,12},{7,13},{8,2},{9,3},... | collective-permute-start | bytes 49160 | tf_op jit(solution)/shard_map/ppermute | solution.py:118
  51.1 1.4 %collective-permute-start.10 = (f32[4,1024]{1,0:T(4,128)S(1)}, f32[4,1024]{1,0:T(4,128)S(1)}, u32[]{:S(2)}, u32[]{:S(2)}) collective-permute-start(f32[4,1024]{1,0:T(4,128)S(1)} %get-tuple-element.235), channel_id=1, source_target_pairs={{0,11},{1,10},{2,9},{3,8},{4,15},{5,14},{6,13},{7,12},{8,3},{9,2},... | collective-permute-start | bytes 49160 | tf_op jit(solution)/shard_map/ppermute | solution.py:118
  52.5 1.2 %collective-permute-start.11 = (f32[4,1024]{1,0:T(4,128)S(1)}, f32[4,1024]{1,0:T(4,128)S(1)}, u32[]{:S(2)}, u32[]{:S(2)}) collective-permute-start(f32[4,1024]{1,0:T(4,128)S(1)} %get-tuple-element.234), channel_id=1, source_target_pairs={{0,12},{1,13},{2,14},{3,15},{4,8},{5,9},{6,10},{7,11},{8,4},{9,5},... | collective-permute-start | bytes 49160 | tf_op jit(solution)/shard_map/ppermute | solution.py:118
  54.3 1.2 %collective-permute-start.13 = (f32[4,1024]{1,0:T(4,128)S(1)}, f32[4,1024]{1,0:T(4,128)S(1)}, u32[]{:S(2)}, u32[]{:S(2)}) collective-permute-start(f32[4,1024]{1,0:T(4,128)S(1)} %get-tuple-element.232), channel_id=1, source_target_pairs={{0,14},{1,15},{2,12},{3,13},{4,10},{5,11},{6,8},{7,9},{8,6},{9,7},... | collective-permute-start | bytes 49160 | tf_op jit(solution)/shard_map/ppermute | solution.py:118
  55.5 1.4 %collective-permute-start.14 = (f32[4,1024]{1,0:T(4,128)S(1)}, f32[4,1024]{1,0:T(4,128)S(1)}, u32[]{:S(2)}, u32[]{:S(2)}) collective-permute-start(f32[4,1024]{1,0:T(4,128)S(1)} %get-tuple-element.231), channel_id=1, source_target_pairs={{0,15},{1,14},{2,13},{3,12},{4,11},{5,10},{6,9},{7,8},{8,7},{9,6},... | collective-permute-start | bytes 49160 | tf_op jit(solution)/shard_map/ppermute | solution.py:118
  57.1 0.7 collective-permute-done.13
  57.8 2.0 %collective-permute-done.14 = f32[4,1024]{1,0:T(4,128)S(1)} collective-permute-done((f32[4,1024]{1,0:T(4,128)S(1)}, f32[4,1024]{1,0:T(4,128)S(1)}, u32[]{:S(2)}, u32[]{:S(2)}) %collective-permute-start.14) | collective-permute-done | bytes 16416 | tf_op jit(solution)/shard_map/ppermute | solution.py:118
  59.8 0.7 gather_fusion
  61.2 14.3 %all_to_all.16 = bf16[4,16,1024]{2,0,1:T(4,128)(2,1)S(1)} all-to-all(bf16[4,16,1024]{2,0,1:T(4,128)(2,1)S(1)} %fusion.11), channel_id=1, replica_groups=mesh['hap'=2,'snp'=16] {'snp'}, dimensions={1} | all-to-all | bytes 262144 | tf_op jit(solution)/shard_map/all_to_all | solution.py:122
  75.6 3.6 %collective-permute-start.15 = (bf16[64,256]{1,0:T(8,128)(2,1)S(1)}, bf16[64,256]{1,0:T(8,128)(2,1)S(1)}, u32[]{:S(2)}, u32[]{:S(2)}) collective-permute-start(bf16[64,256]{1,0:T(8,128)(2,1)S(1)} %get-tuple-element.248), channel_id=1, source_target_pairs={{0,1},{1,2},{2,3},{3,4},{4,5},{5,6},{6,7},{7,8},{8,9},{9,10},{10,1... | collective-permute-start | bytes 98312 | tf_op jit(solution)/shard_map/ppermute | solution.py:29
  79.2 1.9 %collective-permute-start.16 = (bf16[64,256]{1,0:T(8,128)(2,1)S(1)}, bf16[64,256]{1,0:T(8,128)(2,1)S(1)}, u32[]{:S(2)}, u32[]{:S(2)}) collective-permute-start(bf16[64,256]{1,0:T(8,128)(2,1)S(1)} %get-tuple-element.247), channel_id=1, source_target_pairs={{1,0},{2,1},{3,2},{4,3},{5,4},{6,5},{7,6},{8,7},{9,8},{10,9},{11,1... | collective-permute-start | bytes 98312 | tf_op jit(solution)/shard_map/ppermute | solution.py:32
  81.2 4.2 %collective-permute-done.16 = bf16[64,256]{1,0:T(8,128)(2,1)S(1)} collective-permute-done((bf16[64,256]{1,0:T(8,128)(2,1)S(1)}, bf16[64,256]{1,0:T(8,128)(2,1)S(1)}, u32[]{:S(2)}, u32[]{:S(2)}) %collective-permute-start.16) | collective-permute-done | bytes 32800 | tf_op jit(solution)/shard_map/ppermute | solution.py:32
  85.5 0.7 copy-done.1
  86.1 6.3 %while.26 = (s32[]{:T(128)}, f32[2,256]{1,0:T(2,128)S(1)}, s32[2]{0:T(128)S(1)}, s32[]{:T(128)}, s32[]{:T(128)}, /*index=5*/s32[2,1024]{1,0:T(2,128)S(1)}, s32[1...) while((s32[]{:T(128)}, f32[2,256]{1,0:T(2,128)S(1)}, ...), condition=%wide.region_9.10_spmd, body=%wide.region_6.9_spmd.sunk | while | flops 28510736 | bytes 194930 | solution.py:106
  86.1 0.6 dynamic_slice.160
  87.5 0.8 subtract_maximum_fusion.2
  90.6 0.8 subtract_maximum_fusion.2
  92.5 3.2 %all-gather = f32[2,1,512]{2,1,0:T(1,128)S(1)} all-gather(f32[1,1,512]{2,1,0:T(1,128)S(1)} %reshape.123), channel_id=1, replica_groups=mesh['hap'=2,'snp'=16] {'hap'}, dimensions={0}, use_global_device_ids=true | all-gather | bytes 6144 | tf_op jit(solution)/shard_map/all_gather | solution.py:138
  (98 shorter events, 8.7 us)
Async XLA Ops:
  6.5 31.4 %all-reduce.2.cloned.1.call-start = ((), (), s32[]{:S(2)}) async-start(), calls=%async_computation.1 | async-start | bytes 524288 | tf_op jit(solution)/shard_map/psum | solution.py:112
  6.5 0.9 copy-start
  38.9 4.8 %collective-permute-start = (f32[4,1024]{1,0:T(4,128)S(1)}, f32[4,1024]{1,0:T(4,128)S(1)}, u32[]{:S(2)}, u32[]{:S(2)}) collective-permute-start(f32[4,1024]{1,0:T(4,128)S(1)} %get-tuple-element.245), channel_id=1, source_target_pairs={{0,1},{1,0},{2,3},{3,2},{4,5},{5,4},{6,7},{7,6},{8,9},{9,8},{10,11... | collective-permute-start | bytes 49160 | tf_op jit(solution)/shard_map/ppermute | solution.py:118
  40.1 3.8 %collective-permute-start.1 = (f32[4,1024]{1,0:T(4,128)S(1)}, f32[4,1024]{1,0:T(4,128)S(1)}, u32[]{:S(2)}, u32[]{:S(2)}) collective-permute-start(f32[4,1024]{1,0:T(4,128)S(1)} %get-tuple-element.244), channel_id=1, source_target_pairs={{0,2},{1,3},{2,0},{3,1},{4,6},{5,7},{6,4},{7,5},{8,10},{9,11},{10,... | collective-permute-start | bytes 49160 | tf_op jit(solution)/shard_map/ppermute | solution.py:118
  40.4 5.9 %collective-permute-start.2 = (f32[4,1024]{1,0:T(4,128)S(1)}, f32[4,1024]{1,0:T(4,128)S(1)}, u32[]{:S(2)}, u32[]{:S(2)}) collective-permute-start(f32[4,1024]{1,0:T(4,128)S(1)} %get-tuple-element.243), channel_id=1, source_target_pairs={{0,3},{1,2},{2,1},{3,0},{4,7},{5,6},{6,5},{7,4},{8,11},{9,10},{10,... | collective-permute-start | bytes 49160 | tf_op jit(solution)/shard_map/ppermute | solution.py:118
  41.9 6.6 %collective-permute-start.3 = (f32[4,1024]{1,0:T(4,128)S(1)}, f32[4,1024]{1,0:T(4,128)S(1)}, u32[]{:S(2)}, u32[]{:S(2)}) collective-permute-start(f32[4,1024]{1,0:T(4,128)S(1)} %get-tuple-element.242), channel_id=1, source_target_pairs={{0,4},{1,5},{2,6},{3,7},{4,0},{5,1},{6,2},{7,3},{8,12},{9,13},{10,... | collective-permute-start | bytes 49160 | tf_op jit(solution)/shard_map/ppermute | solution.py:118
  42.1 6.9 %collective-permute-start.4 = (f32[4,1024]{1,0:T(4,128)S(1)}, f32[4,1024]{1,0:T(4,128)S(1)}, u32[]{:S(2)}, u32[]{:S(2)}) collective-permute-start(f32[4,1024]{1,0:T(4,128)S(1)} %get-tuple-element.241), channel_id=1, source_target_pairs={{0,5},{1,4},{2,7},{3,6},{4,1},{5,0},{6,3},{7,2},{8,13},{9,12},{10,... | collective-permute-start | bytes 49160 | tf_op jit(solution)/shard_map/ppermute | solution.py:118
  43.6 7.5 %collective-permute-start.5 = (f32[4,1024]{1,0:T(4,128)S(1)}, f32[4,1024]{1,0:T(4,128)S(1)}, u32[]{:S(2)}, u32[]{:S(2)}) collective-permute-start(f32[4,1024]{1,0:T(4,128)S(1)} %get-tuple-element.240), channel_id=1, source_target_pairs={{0,6},{1,7},{2,4},{3,5},{4,2},{5,3},{6,0},{7,1},{8,14},{9,15},{10,... | collective-permute-start | bytes 49160 | tf_op jit(solution)/shard_map/ppermute | solution.py:118
  43.9 8.6 %collective-permute-start.6 = (f32[4,1024]{1,0:T(4,128)S(1)}, f32[4,1024]{1,0:T(4,128)S(1)}, u32[]{:S(2)}, u32[]{:S(2)}) collective-permute-start(f32[4,1024]{1,0:T(4,128)S(1)} %get-tuple-element.239), channel_id=1, source_target_pairs={{0,7},{1,6},{2,5},{3,4},{4,3},{5,2},{6,1},{7,0},{8,15},{9,14},{10,... | collective-permute-start | bytes 49160 | tf_op jit(solution)/shard_map/ppermute | solution.py:118
  46.3 7.5 %collective-permute-start.7 = (f32[4,1024]{1,0:T(4,128)S(1)}, f32[4,1024]{1,0:T(4,128)S(1)}, u32[]{:S(2)}, u32[]{:S(2)}) collective-permute-start(f32[4,1024]{1,0:T(4,128)S(1)} %get-tuple-element.238), channel_id=1, source_target_pairs={{0,8},{1,9},{2,10},{3,11},{4,12},{5,13},{6,14},{7,15},{8,0},{9,1},... | collective-permute-start | bytes 49160 | tf_op jit(solution)/shard_map/ppermute | solution.py:118
  48.4 5.9 %collective-permute-start.8 = (f32[4,1024]{1,0:T(4,128)S(1)}, f32[4,1024]{1,0:T(4,128)S(1)}, u32[]{:S(2)}, u32[]{:S(2)}) collective-permute-start(f32[4,1024]{1,0:T(4,128)S(1)} %get-tuple-element.237), channel_id=1, source_target_pairs={{0,9},{1,8},{2,11},{3,10},{4,13},{5,12},{6,15},{7,14},{8,1},{9,0},... | collective-permute-start | bytes 49160 | tf_op jit(solution)/shard_map/ppermute | solution.py:118
  49.0 6.5 %collective-permute-start.9 = (f32[4,1024]{1,0:T(4,128)S(1)}, f32[4,1024]{1,0:T(4,128)S(1)}, u32[]{:S(2)}, u32[]{:S(2)}) collective-permute-start(f32[4,1024]{1,0:T(4,128)S(1)} %get-tuple-element.236), channel_id=1, source_target_pairs={{0,10},{1,11},{2,8},{3,9},{4,14},{5,15},{6,12},{7,13},{8,2},{9,3},... | collective-permute-start | bytes 49160 | tf_op jit(solution)/shard_map/ppermute | solution.py:118
  51.1 5.9 %collective-permute-start.10 = (f32[4,1024]{1,0:T(4,128)S(1)}, f32[4,1024]{1,0:T(4,128)S(1)}, u32[]{:S(2)}, u32[]{:S(2)}) collective-permute-start(f32[4,1024]{1,0:T(4,128)S(1)} %get-tuple-element.235), channel_id=1, source_target_pairs={{0,11},{1,10},{2,9},{3,8},{4,15},{5,14},{6,13},{7,12},{8,3},{9,2},... | collective-permute-start | bytes 49160 | tf_op jit(solution)/shard_map/ppermute | solution.py:118
  52.5 4.5 %collective-permute-start.11 = (f32[4,1024]{1,0:T(4,128)S(1)}, f32[4,1024]{1,0:T(4,128)S(1)}, u32[]{:S(2)}, u32[]{:S(2)}) collective-permute-start(f32[4,1024]{1,0:T(4,128)S(1)} %get-tuple-element.234), channel_id=1, source_target_pairs={{0,12},{1,13},{2,14},{3,15},{4,8},{5,9},{6,10},{7,11},{8,4},{9,5},... | collective-permute-start | bytes 49160 | tf_op jit(solution)/shard_map/ppermute | solution.py:118
  53.7 3.4 %collective-permute-start.12 = (f32[4,1024]{1,0:T(4,128)S(1)}, f32[4,1024]{1,0:T(4,128)S(1)}, u32[]{:S(2)}, u32[]{:S(2)}) collective-permute-start(f32[4,1024]{1,0:T(4,128)S(1)} %get-tuple-element.233), channel_id=1, source_target_pairs={{0,13},{1,12},{2,15},{3,14},{4,9},{5,8},{6,11},{7,10},{8,5},{9,4},... | collective-permute-start | bytes 49160 | tf_op jit(solution)/shard_map/ppermute | solution.py:118
  54.3 3.5 %collective-permute-start.13 = (f32[4,1024]{1,0:T(4,128)S(1)}, f32[4,1024]{1,0:T(4,128)S(1)}, u32[]{:S(2)}, u32[]{:S(2)}) collective-permute-start(f32[4,1024]{1,0:T(4,128)S(1)} %get-tuple-element.232), channel_id=1, source_target_pairs={{0,14},{1,15},{2,12},{3,13},{4,10},{5,11},{6,8},{7,9},{8,6},{9,7},... | collective-permute-start | bytes 49160 | tf_op jit(solution)/shard_map/ppermute | solution.py:118
  55.5 4.3 %collective-permute-start.14 = (f32[4,1024]{1,0:T(4,128)S(1)}, f32[4,1024]{1,0:T(4,128)S(1)}, u32[]{:S(2)}, u32[]{:S(2)}) collective-permute-start(f32[4,1024]{1,0:T(4,128)S(1)} %get-tuple-element.231), channel_id=1, source_target_pairs={{0,15},{1,14},{2,13},{3,12},{4,11},{5,10},{6,9},{7,8},{8,7},{9,6},... | collective-permute-start | bytes 49160 | tf_op jit(solution)/shard_map/ppermute | solution.py:118
  75.6 5.6 %collective-permute-start.15 = (bf16[64,256]{1,0:T(8,128)(2,1)S(1)}, bf16[64,256]{1,0:T(8,128)(2,1)S(1)}, u32[]{:S(2)}, u32[]{:S(2)}) collective-permute-start(bf16[64,256]{1,0:T(8,128)(2,1)S(1)} %get-tuple-element.248), channel_id=1, source_target_pairs={{0,1},{1,2},{2,3},{3,4},{4,5},{5,6},{6,7},{7,8},{8,9},{9,10},{10,1... | collective-permute-start | bytes 98312 | tf_op jit(solution)/shard_map/ppermute | solution.py:29
  79.2 6.1 %collective-permute-start.16 = (bf16[64,256]{1,0:T(8,128)(2,1)S(1)}, bf16[64,256]{1,0:T(8,128)(2,1)S(1)}, u32[]{:S(2)}, u32[]{:S(2)}) collective-permute-start(bf16[64,256]{1,0:T(8,128)(2,1)S(1)} %get-tuple-element.247), channel_id=1, source_target_pairs={{1,0},{2,1},{3,2},{4,3},{5,4},{6,5},{7,6},{8,7},{9,8},{10,9},{11,1... | collective-permute-start | bytes 98312 | tf_op jit(solution)/shard_map/ppermute | solution.py:32
  85.4 0.7 copy-start.1
Sparse Core Ops, SparseCore 0:
  14.0 23.8 all-reduce.1
